TPU v7x, 128 devices: a whole 4x4x4 slice. The times are simulated.
128 devices in a mesh: dp: 8 (over x, core), rows: 16 (over z, y).
Axes of the slice: x: 4, y: 4, z: 4, core: 2. Of those that a mesh axis runs over, the one named last changes fastest.
Arguments:
- item_table: float32 [524288, 128], P(('dp', 'rows')), may hold values from -3 to 3
- adagrad_state: float32 [524288, 128], P(('dp', 'rows')), may hold values from 0.0001 to 0.01
- history_ids: int32 [16384, 50], P(('dp', 'rows')), may hold values from 0 to 524287, as said below
- positive_ids: int32 [16384], P(('dp', 'rows')), may hold values from 0 to 524287, as said below
Outputs:
- new_table: float32 [524288, 128], P(('dp', 'rows'))
- new_state: float32 [524288, 128], P(('dp', 'rows'))
Inputs may be any that keep to these rules, and one draw needn't show every extreme that they name: `history_ids`: ids are counted over one device's 128 users (an aligned block of users), history and positive together, with repeats. In every such block, at most 128 ids have any one value of id // 4096, and some value has exactly 128; one value has exactly 128 in every block. Popular items repeat. `positive_ids`: counted together with history_ids as stated there.
All inputs are finite; a program needn't handle non-finite values.
Results may differ from a plain program's by a relative error of at most 0.00012.
Values sent between devices are 32-bit elements; how exact they have to be, the bound alone decides.
No kernel may reach another device: no remote copies, remote signals or barrier semaphores. Data moves between devices by JAX's collectives and lax.ppermute only.
A program may use at most 128 MiB of HBM per device.

v0:
```python
import jax
import jax.numpy as jnp
from jax import lax
from jax.sharding import Mesh
from jax.sharding import PartitionSpec as P

DP = ("dp_0", "dp_1")
ROWS = ("rows_0", "rows_1")
DP_ROWS = ("dp_0", "dp_1", "rows_0", "rows_1")
penalty_weight = 10.0
step_size = 0.05


def total_of_pieces(array, axis):
    blocks = lax.all_gather(array, axis)
    return blocks.sum(axis=0)


def one_axis_at_a_time(array, axes):
    for axis in axes:
        array = lax.psum(array, axis)
    return array


def owner_ranks(owner_dev, devices):
    total = owner_dev.shape[0]
    block = min(512, (total + 7) // 8 * 8)
    padded = (total + block - 1) // block * block
    owners_pad = jnp.concatenate([owner_dev, jnp.full((padded - total,), -1, jnp.int32)])
    owner_blocks = owners_pad.reshape(padded // block, block)
    lower = (
        jnp.arange(block, dtype=jnp.int32)[:, None] >= jnp.arange(block, dtype=jnp.int32)[None, :]
    ).astype(jnp.float32)
    columns = jnp.arange(devices, dtype=jnp.int32)[None, :]

    def step(carry, owners_blk):
        member = (owners_blk[:, None] == columns).astype(jnp.float32)
        prefix = jnp.dot(lower, member, preferred_element_type=jnp.float32)
        before = jnp.sum(member * carry[None, :], axis=1)
        ranks = jnp.sum(prefix * member, axis=1) + before - 1.0
        return (carry + jnp.sum(member, axis=0), ranks.astype(jnp.int32))

    start = jnp.zeros((devices,), jnp.float32)
    final, ranks = lax.scan(step, start, owner_blocks)
    return ranks.reshape(-1)[:total]


def shards(item_table, adagrad_state, history_ids, positive_ids):
    rows_dev, width = item_table.shape
    users_dev, hist_len = history_ids.shape
    n_data = lax.axis_size(DP)
    n_shard = lax.axis_size(ROWS)
    devices = n_data * n_shard
    requests = jnp.concatenate([history_ids, positive_ids[:, None]], axis=1).reshape(-1)
    request_count = requests.shape[0]
    capacity = max(8, (request_count * 5 // (2 * devices) + 7) // 8 * 8)
    owner_dev = requests // rows_dev
    local_row = requests % rows_dev
    slot_rank = owner_ranks(owner_dev, devices)
    flat_slot = owner_dev * capacity + slot_rank
    inverse = (
        jnp.full((devices * capacity,), request_count, jnp.int32)
        .at[flat_slot]
        .set(jnp.arange(request_count, dtype=jnp.int32))
    )
    local_pad = jnp.concatenate([local_row, jnp.full((1,), -1, jnp.int32)])
    wanted = jnp.take(local_pad, inverse, axis=0)
    item_gram = jnp.dot(
        item_table.T,
        item_table,
        precision=lax.Precision.HIGHEST,
        preferred_element_type=jnp.float32,
    )
    item_total = total_of_pieces(item_gram, DP_ROWS)
    asked = lax.all_to_all(
        wanted.reshape(devices, capacity), DP_ROWS, split_axis=0, concat_axis=0, tiled=True
    )
    present = asked >= 0
    picked = jnp.take(item_table, jnp.where(present, asked, 0), axis=0)
    fetched_rows = lax.all_to_all(
        picked * present[..., None].astype(jnp.float32),
        DP_ROWS,
        split_axis=0,
        concat_axis=0,
        tiled=True,
    )
    request_rows = jnp.take(
        fetched_rows.reshape(devices * capacity, width), flat_slot, axis=0
    ).reshape(users_dev, hist_len + 1, width)
    user_vecs = jnp.sum(request_rows[:, :hist_len], axis=1) / hist_len
    positive_vecs = request_rows[:, hist_len]
    score_gap = jnp.sum(user_vecs * positive_vecs, axis=1) - 1.0
    user_gram = jnp.dot(
        user_vecs.T, user_vecs, precision=lax.Precision.HIGHEST, preferred_element_type=jnp.float32
    )
    user_total = one_axis_at_a_time(user_gram, DP_ROWS)
    penalty_coef = penalty_weight / (rows_dev * devices)
    user_grad = 2.0 * score_gap[:, None] * positive_vecs + 2.0 * penalty_coef * jnp.dot(
        user_vecs, item_total, precision=lax.Precision.HIGHEST, preferred_element_type=jnp.float32
    )
    positive_grad = 2.0 * score_gap[:, None] * user_vecs
    per_history = jnp.broadcast_to((user_grad / hist_len)[:, None, :], (users_dev, hist_len, width))
    request_grad = jnp.concatenate([per_history, positive_grad[:, None, :]], axis=1).reshape(
        -1, width
    )
    grad_pad = jnp.concatenate([request_grad, jnp.zeros((1, width), jnp.float32)], axis=0)
    outgoing = jnp.take(grad_pad, inverse, axis=0)
    returned = lax.all_to_all(
        outgoing.reshape(devices, capacity, width), DP_ROWS, split_axis=0, concat_axis=0, tiled=True
    )
    present = asked >= 0
    target_rows = jnp.where(present, asked, 0).reshape(-1)
    masked_grad = (returned * present[..., None].astype(jnp.float32)).reshape(-1, width)
    row_grad = (
        2.0
        * penalty_coef
        * jnp.dot(
            item_table,
            user_total,
            precision=lax.Precision.HIGHEST,
            preferred_element_type=jnp.float32,
        )
    )
    row_grad = row_grad.at[target_rows].add(masked_grad)
    new_state = adagrad_state + row_grad * row_grad
    new_table = item_table - step_size * row_grad / jnp.sqrt(new_state)
    return (new_table, new_state)


def solution(mesh):
    finer = Mesh(mesh.devices.reshape(4, 2, 4, 4), ("dp_0", "dp_1", "rows_0", "rows_1"))
    placed = (P(DP_ROWS, None), P(DP_ROWS, None), P(DP_ROWS, None), P(DP_ROWS))
    return jax.shard_map(
        shards,
        mesh=finer,
        in_specs=placed,
        out_specs=(P(DP_ROWS, None), P(DP_ROWS, None)),
        check_vma=False,
    )
```

profile of v0, /device:TPU:0, one launch (start us, length us, event | category | flops | bytes accessed | tf_op | source)
XLA Modules:
  0.0 751.5 jit_solution(16251602117945407127)
XLA Ops:
  8.1 6.3 fusion.34
  14.5 0.2 reshape.200
  14.8 7.9 %while.15 = (s32[]{:T(128)}, f32[128]{0:T(128)S(1)}, s32[13,512]{1,0:T(8,128)S(1)}, s32[13,512]{1,0:T(8,128)S(1)}, s32[]{:T(128)}, /*index=5*/s32[]{:T(128)}) while((s32[]{:T(128)}, f32[128]{0:T(128)S(1)}, s32[13,512]{1,0:T(8,128)S(1)}, s32[13,512]{1,0:T(8,128)S(1)}, s32[]{:T(128)}, /*index=5*/s32[]{:T(128)}) %tuple.43), condition=%wide.region_4.5_spmd.clone, body=%wide.region_0.4_spmd.clone.sunk | while | flops 68223744 | bytes 26200 | solution.py:44
  15.0 0.3 fusion.48
  15.6 0.3 fusion.48
  16.2 0.3 fusion.48
  16.8 0.3 fusion.48
  17.4 0.3 fusion.48
  18.1 0.3 fusion.48
  18.7 0.3 fusion.48
  19.3 0.3 fusion.48
  19.9 0.3 fusion.48
  20.5 0.3 fusion.48
  21.1 0.3 fusion.48
  21.7 0.3 fusion.48
  22.3 0.3 fusion.48
  22.8 31.1 %scatter_custom_fusion = s32[16384]{0:T(1024)S(1)} fusion(s32[6528]{0:T(1024)S(1)} %get-tuple-element.116, s32[6528]{0:T(1024)S(1)} %iota.16, s32[]{:T(128)} %constant.135.clone.1), kind=kCustom, calls=%fused_computation.68 | custom fusion | bytes 65540 | tf_op jit(solution)/shard_map/scatter | solution.py:64
  54.0 90.5 %gather_fusion = s32[16384]{0:T(1024)S(1)} fusion(s32[6529]{0:T(1024)S(1)} %pad_add_fusion.1, s32[16384]{0:T(1024)S(1)} %fusion.20), kind=kCustom, calls=%fused_computation | custom fusion | bytes 196608 | tf_op jit(solution)/shard_map/jit(_take)/gather | solution.py:67
  144.6 20.4 %all_to_all.25 = s32[128,1,128]{2,1,0:T(1,128)S(1)} all-to-all(s32[128,1,128]{2,1,0:T(1,128)S(1)} %bitcast.55), channel_id=1, replica_groups=mesh['dp_0'=4,'dp_1'=2,'rows_0'=4,'rows_1'=4] {'dp_0','dp_1','rows_0','r..., dimensions={0} | all-to-all | bytes 131072 | tf_op jit(solution)/shard_map/all_to_all | solution.py:75
  165.1 54.4 %gather_fusion.1 = f32[16384,128]{1,0:T(8,128)} fusion(f32[4096,128]{1,0:T(8,128)S(1)} %copy-done, s32[16384]{0:T(1024)S(1)} %fusion.16), kind=kCustom, calls=%fused_computation.1 | custom fusion | bytes 16842752 | tf_op jit(solution)/shard_map/jit(_take)/gather | solution.py:79
  219.5 7.5 %select_multiply_fusion = f32[128,128,128]{2,1,0:T(8,128)} fusion(f32[128,128,128]{2,1,0:T(8,128)} %bitcast.48, f32[128,128]{1,0:T(8,128)S(1)} %get-tuple-element.114, pred[128,128]{1,0:T(8,128)(4,1)S(1)} %get-tuple-element.113), kind=kLoop, calls=%fused_computation.22 | loop fusion | flops 4194304 | bytes 16859136 | tf_op jit(solution)/shard_map/mul | solution.py:81
  227.0 5.9 all-to-all-start.1
  233.0 0.2 slice.12
  233.3 106.0 %all-to-all-done.1 = f32[128,128,128]{2,1,0:T(8,128)} async-done(((f32[128,128,128]{2,1,0:T(8,128)}), f32[128,128,128]{2,1,0:T(8,128)}, u32[]{:S(2)}, u32[]{:S(2)}) %all-to-all-start.1) | async-done | bytes 8388640 | tf_op jit(solution)/shard_map/all_to_all | solution.py:80
  339.3 16.3 %gather_fusion.2 = f32[6528,128]{1,0:T(8,128)} fusion(f32[16384,128]{1,0:T(8,128)} %bitcast.6, s32[7168]{0:T(1024)S(1)} %pad_clamp_fusion), kind=kCustom, calls=%fused_computation.2 | custom fusion | bytes 6710784 | tf_op jit(solution)/shard_map/jit(_take)/gather | solution.py:87
  355.6 4.6 gather.23
  360.2 3.6 copy_select_fusion
  363.8 0.2 slice_reduce_fusion
  364.0 1.6 copy-done.1
  365.8 3.8 reduce_sum.67
  369.6 1.0 fusion.14
  370.7 0.2 broadcast_in_dim.90
  370.9 2.1 pad_maximum_fusion
  373.0 4.6 reshape.204
  377.6 4.0 concatenate.19
  381.6 56.4 %gather_fusion.3 = f32[16384,128]{1,0:T(8,128)} fusion(f32[6529,128]{1,0:T(8,128)} %concatenate.19, s32[16384]{0:T(1024)S(1)} %fusion.20), kind=kCustom, calls=%fused_computation.3 | custom fusion | bytes 16842752 | tf_op jit(solution)/shard_map/jit(_take)/gather | solution.py:107
  437.9 9.9 %broadcast_select_fusion.1 = f32[128,128,128]{2,1,0:T(8,128)} fusion(f32[128,128,128]{2,1,0:T(8,128)} %bitcast.49, pred[128,128]{1,0:T(8,128)(4,1)S(1)} %bitcast.59), kind=kLoop, calls=%fused_computation.26 | loop fusion | flops 2097152 | bytes 16793600 | tf_op jit(solution)/shard_map/jit(_take)/select_n | solution.py:107
  447.9 6.1 all-to-all-start.2
  454.0 0.9 fusion.18
  455.0 46.2 %all-reduce.7.cloned.1.call-done = f32[128,128]{1,0:T(8,128)} async-done(((f32[128,128]{1,0:T(8,128)}), f32[128,128]{1,0:T(8,128)}) %all-reduce.7.cloned.1.call-update) | async-done | bytes 65552 | tf_op jit(solution)/shard_map/psum | solution.py:21
  501.3 26.4 %all-reduce.9.cloned.1.call-done = f32[128,128]{1,0:T(8,128)} async-done(((f32[128,128]{1,0:T(8,128)}), f32[128,128]{1,0:T(8,128)}) %all-reduce.9.cloned.1.call-update) | async-done | bytes 65552 | tf_op jit(solution)/shard_map/psum | solution.py:21
  527.7 50.8 %all-reduce.11.cloned.1.call-done = f32[128,128]{1,0:T(8,128)} async-done(((f32[128,128]{1,0:T(8,128)}), f32[128,128]{1,0:T(8,128)}) %all-reduce.11.cloned.1.call-update) | async-done | bytes 65552 | tf_op jit(solution)/shard_map/psum | solution.py:21
  578.6 43.1 %all-reduce.13.cloned.1.call-done = f32[128,128]{1,0:T(8,128)} async-done(((f32[128,128]{1,0:T(8,128)}), f32[128,128]{1,0:T(8,128)}) %all-reduce.13.cloned.1.call-update) | async-done | bytes 65552 | tf_op jit(solution)/shard_map/psum | solution.py:21
  621.7 4.1 fusion.12
  625.8 2.9 copy.27
  628.7 7.9 %broadcast_multiply_fusion = f32[128,128,128]{2,1,0:T(8,128)} fusion(f32[128,128,128]{2,1,0:T(8,128)} %all-to-all-done.2, f32[128,128]{1,0:T(8,128)S(1)} %get-tuple-element.114), kind=kLoop, calls=%fused_computation.25 | loop fusion | flops 2097152 | bytes 16842752 | tf_op jit(solution)/shard_map/mul | solution.py:113
  636.6 102.7 %scatter_fusion = f32[4096,128]{1,0:T(8,128)} fusion(f32[4096,128]{1,0:T(8,128)} %copy.27, s32[16384]{0:T(1024)S(1)} %bitcast.53, f32[16384,128]{1,0:T(8,128)} %bitcast.47), kind=kCustom, calls=%fused_computation.5 | custom fusion | flops 2097152 | bytes 25231360 | tf_op jit(solution)/shard_map/scatter-add | solution.py:124
  739.3 4.6 multiply_subtract_fusion
  (119 shorter events, 4.3 us)
Async XLA Ops:
  8.0 6.4 copy-start.3
  8.0 6.4 copy-start.2
  8.0 357.8 %all-gather.3.cloned.1.call-start = ((), (), s32[]{:S(2)}) async-start(), calls=%async_computation.7 | async-start | bytes 8454144 | tf_op jit(solution)/shard_map/all_gather | solution.py:15
  54.0 111.0 %copy-start = (f32[4096,128]{1,0:T(8,128)S(1)}, f32[4096,128]{1,0:T(8,128)}, u32[]{:S(2)}) copy-start(f32[4096,128]{1,0:T(8,128)} %param.6) | copy-start | bytes 6291460
  227.0 112.3 %all-to-all-start.1 = ((f32[128,128,128]{2,1,0:T(8,128)}), f32[128,128,128]{2,1,0:T(8,128)}, u32[]{:S(2)}, u32[]{:S(2)}) async-start(f32[128,128,128]{2,1,0:T(8,128)} %select_multiply_fusion), calls=%async_computation.1 | async-start | bytes 16777216 | tf_op jit(solution)/shard_map/all_to_all | solution.py:80
  363.8 1.8 copy-start.1
  447.9 180.8 %all-to-all-start.2 = ((f32[128,128,128]{2,1,0:T(8,128)}), f32[128,128,128]{2,1,0:T(8,128)}, u32[]{:S(2)}, u32[]{:S(2)}) async-start(f32[128,128,128]{2,1,0:T(8,128)} %broadcast_select_fusion.1), calls=%async_computation.2 | async-start | bytes 16777216 | tf_op jit(solution)/shard_map/all_to_all | solution.py:108
  454.0 47.2 %all-reduce.7.cloned.1.call-start = ((), (), s32[]{:S(2)}) async-start(), calls=%async_computation.3 | async-start | bytes 131072 | tf_op jit(solution)/shard_map/psum | solution.py:21
  455.0 72.7 %all-reduce.9.cloned.1.call-start = ((), (), s32[]{:S(2)}) async-start(), calls=%async_computation.4 | async-start | bytes 131072 | tf_op jit(solution)/shard_map/psum | solution.py:21
  501.2 77.3 %all-reduce.11.cloned.1.call-start = ((), (), s32[]{:S(2)}) async-start(), calls=%async_computation.5 | async-start | bytes 131072 | tf_op jit(solution)/shard_map/psum | solution.py:21
  527.7 94.0 %all-reduce.13.cloned.1.call-start = ((), (), s32[]{:S(2)}) async-start(), calls=%async_computation.6 | async-start | bytes 131072 | tf_op jit(solution)/shard_map/psum | solution.py:21
Sparse Core Ops, SparseCore 0:
  14.5 72.6 all-gather.2
Sparse Core Ops, SparseCore 1:
  457.3 43.8 all-reduce.6
  503.6 24.0 all-reduce.8
  530.0 48.5 all-reduce.10
  580.8 40.8 all-reduce.12
where the time goes:
time: 753 us; the launch traced here: 752 us
  waiting for transfers between devices  273 us (36%)
  local copies, waits for them, and re-layouts  268 us (36%)
  other arithmetic  145 us (19%)
  blocking collectives  20.4 us (3%)
  matrix products  16.4 us (2%)
  between operations  16 us (2%)
  starting transfers between devices  12.3 us (2%)
    psum x4, waiting for transfers between devices, one_axis_at_a_time(): array = lax.psum(array, axis)  166 us
    all_to_all x1, waiting for transfers between devices, shards(): lax.all_to_all(picked * present[..., None].astype(jnp.float32), DP_ROWS,...  106 us
    scatter-add x1, other arithmetic, shards(): row_grad = row_grad.at[target_rows].add(masked_grad)  103 us
    gather x1, local copies, waits for them, and re-layouts, shards(): wanted = jnp.take(local_pad, inverse, axis=0)  90.5 us
    gather x1, local copies, waits for them, and re-layouts, shards(): outgoing = jnp.take(grad_pad, inverse, axis=0)  56.4 us
    gather x1, local copies, waits for them, and re-layouts, shards(): picked = jnp.take(item_table, jnp.where(present, asked, 0), axis=0)  54.4 us
    scatter x1, local copies, waits for them, and re-layouts, shards(): inverse = jnp.full((devices * capacity,), request_count, jnp.int32).at[fl...  31.1 us
    gather x2, local copies, waits for them, and re-layouts, shards(): jnp.take(fetched_rows.reshape(devices * capacity, width), flat_slot, axis=0)  20.9 us
  transfers between devices with their start and end apart: 7, of which 5 were waited for; matrix products, arithmetic and copies ran while one was open for 30% of the time, Pallas kernels for 0%

commit v1 on v0

--- a/solution.py
+++ b/solution.py
@@ -18,7 +18,7 @@
 
 def one_axis_at_a_time(array, axes):
     for axis in axes:
-        array = lax.psum(array, axis)
+        array = jnp.sum(lax.all_gather(array, axis), axis=0)
     return array
 
 

time: 753 us -> 717 us (0.952)
  waiting for transfers between devices: 273 us -> 106 us
  blocking collectives: 20.4 us -> 154 us
    psum x4 -> x0, waiting for transfers between devices: 166 us -> none  [one_axis_at_a_time(): array = lax.psum(array, axis)]
    all_gather x0 -> x4, blocking collectives: none -> 134 us  [one_axis_at_a_time(): array = jnp.sum(lax.all_gather(array, axis), axis=0)]
  transfers between devices with their start and end apart: 7 -> 3, of which waited for: 5 -> 1; matrix products, arithmetic and copies ran while one was open for 30% -> 31% of each run, Pallas kernels for 0% -> 0%
where the time goes in v1:
time: 717 us; the launch traced here: 716 us
  local copies, waits for them, and re-layouts  268 us (37%)
  blocking collectives  154 us (21%)
  other arithmetic  145 us (20%)
  waiting for transfers between devices  106 us (15%)
  matrix products  15 us (2%)
  between operations  14.3 us (2%)
  starting transfers between devices  12.1 us (2%)
    all_gather x4, blocking collectives, one_axis_at_a_time(): array = jnp.sum(lax.all_gather(array, axis), axis=0)  134 us
    all_to_all x1, waiting for transfers between devices, shards(): lax.all_to_all(picked * present[..., None].astype(jnp.float32), DP_ROWS,...  106 us
    scatter-add x1, other arithmetic, shards(): row_grad = row_grad.at[target_rows].add(masked_grad)  103 us
    gather x1, local copies, waits for them, and re-layouts, shards(): wanted = jnp.take(local_pad, inverse, axis=0)  90.5 us
    gather x1, local copies, waits for them, and re-layouts, shards(): outgoing = jnp.take(grad_pad, inverse, axis=0)  56.4 us
    gather x1, local copies, waits for them, and re-layouts, shards(): picked = jnp.take(item_table, jnp.where(present, asked, 0), axis=0)  54.4 us
    scatter x1, local copies, waits for them, and re-layouts, shards(): inverse = jnp.full((devices * capacity,), request_count, jnp.int32).at[fl...  31.1 us
    gather x2, local copies, waits for them, and re-layouts, shards(): jnp.take(fetched_rows.reshape(devices * capacity, width), flat_slot, axis=0)  20.9 us
  transfers between devices with their start and end apart: 3, of which 1 were waited for; matrix products, arithmetic and copies ran while one was open for 31% of the time, Pallas kernels for 0%

profile of v1, /device:TPU:0, one launch (start us, length us, event | category | flops | bytes accessed | tf_op | source)
XLA Modules:
  0.0 715.5 jit_solution(12176099409696322764)
XLA Ops:
  7.2 6.3 fusion.34
  13.7 0.2 reshape.200
  14.0 7.9 %while.15 = (s32[]{:T(128)}, f32[128]{0:T(128)S(1)}, s32[13,512]{1,0:T(8,128)S(1)}, s32[13,512]{1,0:T(8,128)S(1)}, s32[]{:T(128)}, /*index=5*/s32[]{:T(128)}) while((s32[]{:T(128)}, f32[128]{0:T(128)S(1)}, s32[13,512]{1,0:T(8,128)S(1)}, s32[13,512]{1,0:T(8,128)S(1)}, s32[]{:T(128)}, /*index=5*/s32[]{:T(128)}) %tuple.43), condition=%wide.region_4.5_spmd.clone, body=%wide.region_0.4_spmd.clone.sunk | while | flops 68223744 | bytes 26200 | solution.py:44
  14.2 0.3 fusion.48
  14.8 0.3 fusion.48
  15.4 0.3 fusion.48
  16.0 0.3 fusion.48
  16.6 0.3 fusion.48
  17.2 0.3 fusion.48
  17.8 0.3 fusion.48
  18.4 0.3 fusion.48
  19.1 0.3 fusion.48
  19.7 0.3 fusion.48
  20.3 0.3 fusion.48
  20.9 0.3 fusion.48
  21.5 0.3 fusion.48
  22.0 31.1 %scatter_custom_fusion = s32[16384]{0:T(1024)S(1)} fusion(s32[6528]{0:T(1024)S(1)} %get-tuple-element.116, s32[6528]{0:T(1024)S(1)} %iota.16, s32[]{:T(128)} %constant.135.clone.1), kind=kCustom, calls=%fused_computation.68 | custom fusion | bytes 65540 | tf_op jit(solution)/shard_map/scatter | solution.py:64
  53.2 90.5 %gather_fusion = s32[16384]{0:T(1024)S(1)} fusion(s32[6529]{0:T(1024)S(1)} %pad_add_fusion.1, s32[16384]{0:T(1024)S(1)} %fusion.20), kind=kCustom, calls=%fused_computation | custom fusion | bytes 196608 | tf_op jit(solution)/shard_map/jit(_take)/gather | solution.py:67
  143.8 20.4 %all_to_all.25 = s32[128,1,128]{2,1,0:T(1,128)S(1)} all-to-all(s32[128,1,128]{2,1,0:T(1,128)S(1)} %bitcast.63), channel_id=1, replica_groups=mesh['dp_0'=4,'dp_1'=2,'rows_0'=4,'rows_1'=4] {'dp_0','dp_1','rows_0','r..., dimensions={0} | all-to-all | bytes 131072 | tf_op jit(solution)/shard_map/all_to_all | solution.py:75
  164.2 54.4 %gather_fusion.1 = f32[16384,128]{1,0:T(8,128)} fusion(f32[4096,128]{1,0:T(8,128)S(1)} %copy-done, s32[16384]{0:T(1024)S(1)} %fusion.16), kind=kCustom, calls=%fused_computation.1 | custom fusion | bytes 16842752 | tf_op jit(solution)/shard_map/jit(_take)/gather | solution.py:79
  218.7 7.5 %select_multiply_fusion = f32[128,128,128]{2,1,0:T(8,128)} fusion(f32[128,128,128]{2,1,0:T(8,128)} %bitcast.52, f32[128,128]{1,0:T(8,128)S(1)} %get-tuple-element.114, pred[128,128]{1,0:T(8,128)(4,1)S(1)} %get-tuple-element.113), kind=kLoop, calls=%fused_computation.22 | loop fusion | flops 4194304 | bytes 16859136 | tf_op jit(solution)/shard_map/mul | solution.py:81
  226.2 5.9 all-to-all-start.1
  232.1 0.2 slice.12
  232.5 106.0 %all-to-all-done.1 = f32[128,128,128]{2,1,0:T(8,128)} async-done(((f32[128,128,128]{2,1,0:T(8,128)}), f32[128,128,128]{2,1,0:T(8,128)}, u32[]{:S(2)}, u32[]{:S(2)}) %all-to-all-start.1) | async-done | bytes 8388640 | tf_op jit(solution)/shard_map/all_to_all | solution.py:80
  338.5 16.3 %gather_fusion.2 = f32[6528,128]{1,0:T(8,128)} fusion(f32[16384,128]{1,0:T(8,128)} %bitcast.6, s32[7168]{0:T(1024)S(1)} %pad_clamp_fusion), kind=kCustom, calls=%fused_computation.2 | custom fusion | bytes 6710784 | tf_op jit(solution)/shard_map/jit(_take)/gather | solution.py:87
  354.8 4.6 gather.23
  359.4 3.6 copy_select_fusion
  363.0 0.2 slice_reduce_fusion
  363.1 1.6 copy-done.1
  365.0 3.8 reduce_sum.107
  368.8 1.0 fusion.14
  369.8 0.2 broadcast_in_dim.90
  370.1 2.1 pad_maximum_fusion
  372.2 4.6 reshape.204
  376.8 4.0 concatenate.19
  380.7 56.4 %gather_fusion.3 = f32[16384,128]{1,0:T(8,128)} fusion(f32[6529,128]{1,0:T(8,128)} %concatenate.19, s32[16384]{0:T(1024)S(1)} %fusion.20), kind=kCustom, calls=%fused_computation.3 | custom fusion | bytes 16842752 | tf_op jit(solution)/shard_map/jit(_take)/gather | solution.py:107
  437.1 9.9 %broadcast_select_fusion.1 = f32[128,128,128]{2,1,0:T(8,128)} fusion(f32[128,128,128]{2,1,0:T(8,128)} %bitcast.53, pred[128,128]{1,0:T(8,128)(4,1)S(1)} %bitcast.67), kind=kLoop, calls=%fused_computation.26 | loop fusion | flops 2097152 | bytes 16793600 | tf_op jit(solution)/shard_map/jit(_take)/select_n | solution.py:107
  447.0 6.1 all-to-all-start.2
  453.3 0.3 fusion.18
  453.5 103.2 %all-gather = f32[512,128]{1,0:T(8,128)S(1)} all-gather(f32[128,128]{1,0:T(8,128)S(1)} %fusion.18), channel_id=2, replica_groups=mesh['dp_0'=4,'dp_1'=2,'rows_0'=4,'rows_1'=4] {'dp_0'}, dimensions={0}, use_global_device_ids=true | all-gather | bytes 327680 | tf_op jit(solution)/shard_map/all_gather | solution.py:21
  556.8 1.9 all-gather.1
  558.7 15.0 %all-gather.2 = f32[512,128]{1,0:T(8,128)S(1)} all-gather(f32[128,128]{1,0:T(8,128)S(1)} %reduce_sum.103), channel_id=4, replica_groups=mesh['dp_0'=4,'dp_1'=2,'rows_0'=4,'rows_1'=4] {'rows_0'}, dimensions={0}, use_global_device_ids=true | all-gather | bytes 327680 | tf_op jit(solution)/shard_map/all_gather | solution.py:21
  573.7 13.5 %all-gather.3 = f32[512,128]{1,0:T(8,128)S(1)} all-gather(f32[128,128]{1,0:T(8,128)S(1)} %reduce_sum.104), channel_id=5, replica_groups=mesh['dp_0'=4,'dp_1'=2,'rows_0'=4,'rows_1'=4] {'rows_1'}, dimensions={0}, use_global_device_ids=true | all-gather | bytes 327680 | tf_op jit(solution)/shard_map/all_gather | solution.py:21
  587.3 3.3 fusion.12
  590.6 2.9 copy.36
  593.4 7.9 %broadcast_multiply_fusion = f32[128,128,128]{2,1,0:T(8,128)} fusion(f32[128,128,128]{2,1,0:T(8,128)} %all-to-all-done.2, f32[128,128]{1,0:T(8,128)S(1)} %get-tuple-element.114), kind=kLoop, calls=%fused_computation.25 | loop fusion | flops 2097152 | bytes 16842752 | tf_op jit(solution)/shard_map/mul | solution.py:113
  601.3 102.7 %scatter_fusion = f32[4096,128]{1,0:T(8,128)} fusion(f32[4096,128]{1,0:T(8,128)} %copy.36, s32[16384]{0:T(1024)S(1)} %bitcast.61, f32[16384,128]{1,0:T(8,128)} %bitcast.51), kind=kCustom, calls=%fused_computation.5 | custom fusion | flops 2097152 | bytes 25231360 | tf_op jit(solution)/shard_map/scatter-add | solution.py:124
  704.0 4.6 multiply_subtract_fusion
  (115 shorter events, 4.1 us)
Async XLA Ops:
  7.2 6.4 copy-start.3
  7.2 6.4 copy-start.2
  7.2 357.8 %all-gather.7.cloned.1.call-start = ((), (), s32[]{:S(2)}) async-start(), calls=%async_computation.3 | async-start | bytes 8454144 | tf_op jit(solution)/shard_map/all_gather | solution.py:15
  53.2 111.1 %copy-start = (f32[4096,128]{1,0:T(8,128)S(1)}, f32[4096,128]{1,0:T(8,128)}, u32[]{:S(2)}) copy-start(f32[4096,128]{1,0:T(8,128)} %param.6) | copy-start | bytes 6291460
  226.2 112.3 %all-to-all-start.1 = ((f32[128,128,128]{2,1,0:T(8,128)}), f32[128,128,128]{2,1,0:T(8,128)}, u32[]{:S(2)}, u32[]{:S(2)}) async-start(f32[128,128,128]{2,1,0:T(8,128)} %select_multiply_fusion), calls=%async_computation.1 | async-start | bytes 16777216 | tf_op jit(solution)/shard_map/all_to_all | solution.py:80
  362.9 1.8 copy-start.1
  447.0 146.4 %all-to-all-start.2 = ((f32[128,128,128]{2,1,0:T(8,128)}), f32[128,128,128]{2,1,0:T(8,128)}, u32[]{:S(2)}, u32[]{:S(2)}) async-start(f32[128,128,128]{2,1,0:T(8,128)} %broadcast_select_fusion.1), calls=%async_computation.2 | async-start | bytes 16777216 | tf_op jit(solution)/shard_map/all_to_all | solution.py:108
Sparse Core Ops, SparseCore 0:
  13.7 72.6 all-gather.6
